TPU v7x, 128 devices: a whole 4x4x4 slice. The times are simulated.
128 devices in a mesh: tm: 8 (over y_lo, x), chan: 16 (over z, y_hi, core).
Axes of the slice: x: 4, y: 4 (y_hi: 2, y_lo: 2; y = y_hi * 2 + y_lo), z: 4, core: 2. Of those that a mesh axis runs over, the one named last changes fastest.
Arguments:
- samples: bfloat16 [1024, 262144], P('tm', 'chan'), may hold values from -6 to 6
- valid: int32 [1024, 32], P('tm', 'chan'), may hold values from 0 to 1, as said below
Outputs:
- average: float32 [1024, 4224], P(('tm', 'chan'))
Inputs may be any that keep to these rules, and one draw needn't show every extreme that they name: `valid`: split the channels into aligned groups of 128; in every segment each group has at most 96 entries equal to 1, and exactly 96 for some group and segment; at least one channel has no 1 in any segment.
All inputs are finite; a program needn't handle non-finite values.
Results may differ from a plain program's by a relative error of at most 0.0026.
Values may be sent and summed in bfloat16 or wider, within the bound.
A program may use at most 128 MiB of HBM per device.

v0:
```python
import jax
import jax.numpy as jnp
from jax import lax
from jax.sharding import PartitionSpec as P

RADIX = 128
KBANDS = 33


full_turn = 6.283185307179586


def make_tables():
    seg_len = RADIX * RADIX
    counter = jnp.arange(RADIX, dtype=jnp.int32)
    inner_prod = counter[:, None] * counter[None, :] % RADIX
    angle_one = full_turn * inner_prod.astype(jnp.float32) / RADIX
    cos_one = jnp.cos(angle_one).astype(jnp.bfloat16)
    sin_one = jnp.sin(angle_one).astype(jnp.bfloat16)
    outer_prod = counter[:, None] * counter[None, :] % seg_len
    angle_mid = full_turn * outer_prod.astype(jnp.float32) / seg_len
    twid_real = jnp.cos(angle_mid)
    twid_imag = -jnp.sin(angle_mid)
    band_index = jnp.arange(KBANDS, dtype=jnp.int32)
    angle_two = (
        full_turn * (counter[:, None] * band_index[None, :] % RADIX).astype(jnp.float32) / RADIX
    )
    cos_two = jnp.cos(angle_two).astype(jnp.bfloat16)
    sine_double_angle = jnp.sin(angle_two).astype(jnp.bfloat16)
    places = jnp.arange(seg_len, dtype=jnp.int32).astype(jnp.float32)
    window = 0.5 - 0.5 * jnp.cos(full_turn * places / seg_len)
    weight_sum = jnp.sum(window * window)
    onesided = (
        jnp.where(jnp.arange(KBANDS * RADIX, dtype=jnp.int32) == 0, 1.0, 2.0).astype(jnp.float32)
        / weight_sum
    )
    return (cos_one, sin_one, twid_real, twid_imag, cos_two, sine_double_angle, window, onesided)


def contract(left, right, form):
    return jnp.einsum(form, left, right, preferred_element_type=jnp.float32)


def spectrum(segment, tables):
    cos_one, sin_one, twid_real, twid_imag, cos_two, sine_double_angle, window, onesided = tables
    height = segment.shape[0]
    values = segment.astype(jnp.float32)
    centred = values - jnp.mean(values, axis=1, keepdims=True)
    shaped = (centred * window[None, :]).astype(jnp.bfloat16).reshape(height, RADIX, RADIX)
    first_real = contract(shaped, cos_one, "cnm,nk->ckm")
    first_imag = -contract(shaped, sin_one, "cnm,nk->ckm")
    mid_real = (first_real * twid_real - first_imag * twid_imag).astype(jnp.bfloat16)
    mid_imag = (first_real * twid_imag + first_imag * twid_real).astype(jnp.bfloat16)
    last_real = contract(mid_real, cos_two, "ckn,nm->cmk") + contract(
        mid_imag, sine_double_angle, "ckn,nm->cmk"
    )
    closing_quadrature_part = contract(mid_imag, cos_two, "ckn,nm->cmk") - contract(
        mid_real, sine_double_angle, "ckn,nm->cmk"
    )
    return (last_real * last_real + closing_quadrature_part * closing_quadrature_part).reshape(
        height, -1
    ) * onesided[None, :]


def block_power(leading, trailing, tables):
    height = leading.shape[0]
    block_rows = 128
    segments = jnp.concatenate([leading, trailing], axis=1)

    def one_block(piece):
        return spectrum(piece, tables)

    final_output = lax.map(one_block, segments.reshape(height // block_rows, block_rows, -1))
    return final_output.reshape(height, -1)


def per_device(samples, valid):
    tables = make_tables()
    half_len = RADIX * RADIX // 2
    moved_samples, moved_valid = (
        lax.all_to_all(samples, "chan", split_axis=0, concat_axis=1, tiled=True),
        lax.all_to_all(valid.astype(jnp.bfloat16), "chan", split_axis=0, concat_axis=1, tiled=True),
    )
    owned_rows = moved_samples.shape[0]
    record = jnp.concatenate(
        [moved_samples, jnp.zeros((owned_rows, half_len), jnp.bfloat16)], axis=1
    )
    blocks = record.reshape(owned_rows, -1, half_len)
    leading = blocks[:, :-1].reshape(-1, half_len)
    trailing = blocks[:, 1:].reshape(-1, half_len)
    powers = block_power(leading, trailing, tables).reshape(owned_rows, blocks.shape[1] - 1, -1)
    weights = moved_valid.astype(jnp.float32)
    totals = jnp.sum(weights[:, :, None] * powers, axis=1)
    tallied_count = jnp.sum(weights, axis=1)
    return totals / jnp.maximum(tallied_count, 1.0)[:, None]


def solution(mesh):
    return jax.shard_map(
        per_device,
        mesh=mesh,
        in_specs=(P("tm", "chan"), P("tm", "chan")),
        out_specs=P(("tm", "chan"), None),
        check_vma=False,
    )
```

profile of v0, /device:TPU:1, one launch (start us, length us, event | category | flops | bytes accessed | tf_op | source)
XLA Modules:
  0.0 189.5 jit_solution(12834739281329465822)
XLA Ops:
  0.0 0.7 convert_element_type.84
  0.8 16.3 %all_to_all.32 = bf16[16,8,2]{1,2,0:T(2,128)(2,1)S(1)} all-to-all(bf16[16,8,2]{1,2,0:T(2,128)(2,1)S(1)} %copy.36), channel_id=1, replica_groups=mesh['tm'=8,'chan'=16] {'chan'}, dimensions={0} | all-to-all | bytes 1024 | tf_op jit(solution)/shard_map/all_to_all | solution.py:82
  17.1 4.9 %all-to-all-start.1 = ((bf16[16,8,16384]{2,1,0:T(8,128)(2,1)}), bf16[16,8,16384]{2,1,0:T(8,128)(2,1)}, u32[]{:S(2)}, u32[]{:S(2)}) async-start(bf16[16,8,16384]{2,1,0:T(8,128)(2,1)} %bitcast.100), calls=%async_computation.1 | async-start | bytes 8388608 | tf_op jit(solution)/shard_map/all_to_all | solution.py:81
  22.0 0.8 multiply_reduce_fusion.1
  22.8 0.7 copy.37
  23.5 0.5 broadcast_maximum_fusion
  24.0 49.0 %all-to-all-done.1 = bf16[16,8,16384]{2,1,0:T(8,128)(2,1)} async-done(((bf16[16,8,16384]{2,1,0:T(8,128)(2,1)}), bf16[16,8,16384]{2,1,0:T(8,128)(2,1)}, u32[]{:S(2)}, u32[]{:S(2)}) %all-to-all-start.1) | async-done | bytes 4194336 | tf_op jit(solution)/shard_map/all_to_all | solution.py:81
  73.0 3.0 %concatenate.11 = bf16[8,270336]{1,0:T(8,128)(2,1)S(1)} pad(bf16[8,262144]{1,0:T(8,128)(2,1)} %bitcast.4, bf16[]{:T(256)} %constant.69.clone.1), padding=0_0x0_8192 | pad | bytes 8519682 | tf_op jit(solution)/shard_map/concatenate | solution.py:85
  76.0 0.9 fusion.80
  77.0 4.3 %copy.38 = bf16[8,32,8192]{2,1,0:T(8,128)(2,1)} copy(bf16[8,32,8192]{2,0,1:T(8,128)(2,1)S(1)} %get-tuple-element.140) | data formatting | bytes 8388608 | tf_op jit(solution)/shard_map/slice | solution.py:89
  81.2 4.3 %copy.39 = bf16[8,32,8192]{2,1,0:T(8,128)(2,1)} copy(bf16[8,32,8192]{2,0,1:T(8,128)(2,1)S(1)} %get-tuple-element.141) | data formatting | bytes 8388608 | tf_op jit(solution)/shard_map/slice | solution.py:90
  85.5 7.6 %pad_maximum_fusion = bf16[2,128,16384]{2,1,0:T(8,128)(2,1)} fusion(bf16[2,128,8192]{2,1,0:T(8,128)(2,1)} %bitcast.98, bf16[2,128,8192]{2,1,0:T(8,128)(2,1)} %bitcast.97), kind=kLoop, calls=%fused_computation.92 | loop fusion | flops 16777216 | bytes 16777216 | tf_op jit(solution)/shard_map/concatenate | solution.py:68
  93.1 92.8 %while.12 = (s32[]{:T(128)}, f32[2,128,4224]{2,1,0:T(8,128)}, bf16[2,128,16384]{2,1,0:T(8,128)(2,1)}, f32[]{:T(128)}, s32[]{:T(128)}) while((s32[]{:T(128)}, f32[2,128,4224]{2,1,0:T(8,128)}, bf16[2,128,16384]{2,1,0:T(8,128)(2,1)}, f32[]{:T(128)}, s32[]{:T(128)}) %tuple.31), condition=%wide.region_3.4_spmd.clone.clone, body=%wide.region_1.3_spmd.clone.clone.sunk | while | flops 1669451648 | bytes 142118992 | solution.py:73
  93.1 3.0 %convert_bitcast_fusion.2 = f32[16,8,128,128]{3,1,2,0:T(8,128)S(1)} fusion(bf16[2,128,16384]{2,1,0:T(8,128)(2,1)} %get-tuple-element.187, s32[]{:T(128)} %get-tuple-element.180), kind=kLoop, calls=%fused_computation.9.clone.1 | loop fusion | flops 2097152 | bytes 12582916 | tf_op jit(solution)/shard_map/while
  96.1 4.7 %copy.56 = f32[16,8,128,128]{3,2,1,0:T(8,128)} copy(f32[16,8,128,128]{3,1,2,0:T(8,128)S(1)} %convert_bitcast_fusion.2) | data formatting | bytes 16777216 | tf_op jit(solution)/shard_map/while
  100.8 9.0 %copy.57 = f32[128,128,128]{1,2,0:T(8,128)} copy(f32[128,128,128]{2,1,0:T(8,128)} %bitcast.95) | data formatting | bytes 16777216 | tf_op jit(solution)/shard_map/while/body/eval_jaxpr/convert_element_type | solution.py:47
  109.8 2.8 %convert_reduce_fusion.3 = f32[128]{0:T(128)S(1)} fusion(bf16[2,128,16384]{2,1,0:T(8,128)(2,1)} %get-tuple-element.187, s32[]{:T(128)} %get-tuple-element.180), kind=kLoop, calls=%fused_computation.8.clone.1 | loop fusion | flops 4194176 | bytes 4194820 | tf_op jit(solution)/shard_map/while/body/eval_jaxpr/reduce_sum | solution.py:48
  112.6 0.2 subtract_bitcast_fusion.2
  112.9 4.9 %fusion.108 = f32[128,128,128]{2,1,0:T(8,128)S(1)} fusion(f32[128,128,128]{1,2,0:T(8,128)} %copy.57, f32[128,128]{0,1:T(8,128)S(1)} %copy.58, f32[128]{0:T(128)S(1)} %broadcast_multiply_fusion.2), kind=kOutput, calls=%fused_computation.46.clone.1 | convolution fusion | flops 543408128 | bytes 16843264 | tf_op jit(solution)/shard_map/while/body/eval_jaxpr/cnm,nk->ckm/dot_general | solution.py:41
  117.8 0.3 sine_negate_fusion.2
  118.1 7.1 %fusion.109 = (bf16[128,128,128]{1,2,0:T(8,128)(2,1)S(1)}, bf16[128,128,128]{1,2,0:T(8,128)(2,1)S(1)}) fusion(f32[128,128,128]{2,1,0:T(8,128)S(1)} %fusion.108, f32[128,128]{0,1:T(8,128)S(1)} %get-tuple-element.171, f32[128,128]{0,1:T(8,128)S(1)} %get-tuple-element.172, f32[128,128,128]{1,2,0:T(8,128)} %copy.57, f32[128,128]{0,1:T(8,128)S(1)} %copy.58, ...), kind=kOutput, calls=%fused_computation.13.clone.1 | convolution fusion | flops 562282496 | bytes 25362944 | tf_op jit(solution)/shard_map/while/body/eval_jaxpr/cnm,nk->ckm/dot_general | solution.py:41
  125.3 0.7 fusion.110
  126.0 0.8 fusion.111
  126.8 0.8 fusion.112
  127.5 1.0 add_bitcast_fusion.2
  128.6 2.1 %copy.59 = f32[128,33,128]{0,2,1:T(8,128)} copy(f32[128,33,128]{2,1,0:T(8,128)S(1)} %add_bitcast_fusion.2) | data formatting | bytes 4325376 | tf_op jit(solution)/shard_map/while/body/eval_jaxpr/add | solution.py:60
  130.6 0.6 select_divide_fusion.2
  131.3 3.0 %bitcast_multiply_fusion.6 = f32[1,128,4224]{1,2,0:T(8,128)S(1)} fusion(f32[128,33,128]{0,2,1:T(8,128)} %copy.59, f32[4224]{0:T(1024)S(1)} %select_divide_fusion.2), kind=kLoop, calls=%fused_computation.20.clone.1 | loop fusion | flops 540672 | bytes 4342272 | tf_op jit(solution)/shard_map/while/body/eval_jaxpr/mul | solution.py:60
  134.3 2.1 %copy.60 = f32[1,128,4224]{2,1,0:T(8,128)} copy(f32[1,128,4224]{1,2,0:T(8,128)S(1)} %bitcast_multiply_fusion.6) | data formatting | bytes 4325376 | tf_op jit(solution)/shard_map/while/body/jit(dynamic_update_index_in_dim)/dynamic_update_slice | solution.py:73
  136.4 3.1 %constant_dynamic-update-slice_fusion.2 = f32[2,128,4224]{2,1,0:T(8,128)} fusion(f32[2,128,4224]{2,1,0:T(8,128)} %get-tuple-element.181, f32[1,128,4224]{2,1,0:T(8,128)} %copy.60, s32[]{:T(128)} %get-tuple-element.180), kind=kLoop, calls=%fused_computation.72.clone.1 | loop fusion | bytes 4325888 | tf_op jit(solution)/shard_map/while/body/jit(dynamic_update_index_in_dim)/dynamic_update_slice | solution.py:73
  139.5 3.0 %convert_bitcast_fusion.2 = f32[16,8,128,128]{3,1,2,0:T(8,128)S(1)} fusion(bf16[2,128,16384]{2,1,0:T(8,128)(2,1)} %get-tuple-element.187, s32[]{:T(128)} %get-tuple-element.180), kind=kLoop, calls=%fused_computation.9.clone.1 | loop fusion | flops 2097152 | bytes 12582916 | tf_op jit(solution)/shard_map/while
  142.5 4.7 %copy.56 = f32[16,8,128,128]{3,2,1,0:T(8,128)} copy(f32[16,8,128,128]{3,1,2,0:T(8,128)S(1)} %convert_bitcast_fusion.2) | data formatting | bytes 16777216 | tf_op jit(solution)/shard_map/while
  147.2 9.0 %copy.57 = f32[128,128,128]{1,2,0:T(8,128)} copy(f32[128,128,128]{2,1,0:T(8,128)} %bitcast.95) | data formatting | bytes 16777216 | tf_op jit(solution)/shard_map/while/body/eval_jaxpr/convert_element_type | solution.py:47
  156.2 2.8 %convert_reduce_fusion.3 = f32[128]{0:T(128)S(1)} fusion(bf16[2,128,16384]{2,1,0:T(8,128)(2,1)} %get-tuple-element.187, s32[]{:T(128)} %get-tuple-element.180), kind=kLoop, calls=%fused_computation.8.clone.1 | loop fusion | flops 4194176 | bytes 4194820 | tf_op jit(solution)/shard_map/while/body/eval_jaxpr/reduce_sum | solution.py:48
  159.4 4.9 %fusion.108 = f32[128,128,128]{2,1,0:T(8,128)S(1)} fusion(f32[128,128,128]{1,2,0:T(8,128)} %copy.57, f32[128,128]{0,1:T(8,128)S(1)} %copy.58, f32[128]{0:T(128)S(1)} %broadcast_multiply_fusion.2), kind=kOutput, calls=%fused_computation.46.clone.1 | convolution fusion | flops 543408128 | bytes 16843264 | tf_op jit(solution)/shard_map/while/body/eval_jaxpr/cnm,nk->ckm/dot_general | solution.py:41
  164.3 0.3 sine_negate_fusion.2
  164.6 7.1 %fusion.109 = (bf16[128,128,128]{1,2,0:T(8,128)(2,1)S(1)}, bf16[128,128,128]{1,2,0:T(8,128)(2,1)S(1)}) fusion(f32[128,128,128]{2,1,0:T(8,128)S(1)} %fusion.108, f32[128,128]{0,1:T(8,128)S(1)} %get-tuple-element.171, f32[128,128]{0,1:T(8,128)S(1)} %get-tuple-element.172, f32[128,128,128]{1,2,0:T(8,128)} %copy.57, f32[128,128]{0,1:T(8,128)S(1)} %copy.58, ...), kind=kOutput, calls=%fused_computation.13.clone.1 | convolution fusion | flops 562282496 | bytes 25362944 | tf_op jit(solution)/shard_map/while/body/eval_jaxpr/cnm,nk->ckm/dot_general | solution.py:41
  171.7 0.7 fusion.110
  172.4 0.8 fusion.111
  173.2 0.8 fusion.112
  173.9 1.0 add_bitcast_fusion.2
  175.0 2.1 %copy.59 = f32[128,33,128]{0,2,1:T(8,128)} copy(f32[128,33,128]{2,1,0:T(8,128)S(1)} %add_bitcast_fusion.2) | data formatting | bytes 4325376 | tf_op jit(solution)/shard_map/while/body/eval_jaxpr/add | solution.py:60
  177.1 0.6 select_divide_fusion.2
  177.7 3.0 %bitcast_multiply_fusion.6 = f32[1,128,4224]{1,2,0:T(8,128)S(1)} fusion(f32[128,33,128]{0,2,1:T(8,128)} %copy.59, f32[4224]{0:T(1024)S(1)} %select_divide_fusion.2), kind=kLoop, calls=%fused_computation.20.clone.1 | loop fusion | flops 540672 | bytes 4342272 | tf_op jit(solution)/shard_map/while/body/eval_jaxpr/mul | solution.py:60
  180.7 2.1 %copy.60 = f32[1,128,4224]{2,1,0:T(8,128)} copy(f32[1,128,4224]{1,2,0:T(8,128)S(1)} %bitcast_multiply_fusion.6) | data formatting | bytes 4325376 | tf_op jit(solution)/shard_map/while/body/jit(dynamic_update_index_in_dim)/dynamic_update_slice | solution.py:73
  182.8 3.1 %constant_dynamic-update-slice_fusion.2 = f32[2,128,4224]{2,1,0:T(8,128)} fusion(f32[2,128,4224]{2,1,0:T(8,128)} %get-tuple-element.181, f32[1,128,4224]{2,1,0:T(8,128)} %copy.60, s32[]{:T(128)} %get-tuple-element.180), kind=kLoop, calls=%fused_computation.72.clone.1 | loop fusion | bytes 4325888 | tf_op jit(solution)/shard_map/while/body/jit(dynamic_update_index_in_dim)/dynamic_update_slice | solution.py:73
  185.9 2.8 %multiply_reduce_fusion = f32[8,4224]{1,0:T(8,128)S(1)} fusion(f32[8,32,4224]{2,1,0:T(8,128)} %bitcast.99, f32[8,32]{1,0:T(8,128)S(1)} %copy-done), kind=kLoop, calls=%fused_computation.93 | loop fusion | flops 2128896 | bytes 4461568 | tf_op jit(solution)/shard_map/reduce_sum | solution.py:93
  188.8 0.7 broadcast_divide_fusion
  (14 shorter events, 0.6 us)
Async XLA Ops:
  17.1 55.9 %all-to-all-start.1 = ((bf16[16,8,16384]{2,1,0:T(8,128)(2,1)}), bf16[16,8,16384]{2,1,0:T(8,128)(2,1)}, u32[]{:S(2)}, u32[]{:S(2)}) async-start(bf16[16,8,16384]{2,1,0:T(8,128)(2,1)} %bitcast.100), calls=%async_computation.1 | async-start | bytes 8388608 | tf_op jit(solution)/shard_map/all_to_all | solution.py:81
  93.1 92.9 %copy-start = (f32[8,32]{1,0:T(8,128)S(1)}, f32[8,32]{1,0:T(8,128)}, u32[]{:S(2)}) copy-start(f32[8,32]{1,0:T(8,128)} %copy.37) | copy-start | bytes 3076
  185.9 2.8 %copy-start.1 = (f32[8]{0:T(128)S(1)}, f32[8]{0:T(128)}, u32[]{:S(2)}) copy-start(f32[8]{0:T(128)} %broadcast_maximum_fusion) | copy-start | bytes 100
where the time goes:
time: 191 us; the launch traced here: 189 us
  local copies, waits for them, and re-layouts  55.3 us (29%)
  waiting for transfers between devices  49 us (26%)
  other arithmetic  33.2 us (17%)
  matrix products  30.6 us (16%)
  blocking collectives  16.3 us (9%)
  starting transfers between devices  4.93 us (3%)
    all_to_all x1, waiting for transfers between devices, per_device(): lax.all_to_all(samples, 'chan', split_axis=0, concat_axis=1, tiled=True)  49 us
    dot_general x12, matrix products, contract(): return jnp.einsum(form, left, right, preferred_element_type=jnp.float32)  30.6 us
    convert_element_type x2, local copies, waits for them, and re-layouts, spectrum(): values = segment.astype(jnp.float32)  18 us
    all_to_all x1, blocking collectives, per_device(): lax.all_to_all(valid.astype(jnp.bfloat16), 'chan', split_axis=0, concat_a...  16.3 us
    dynamic_update_slice x4, local copies, waits for them, and re-layouts, block_power(): lax.map(one_block, segments.reshape(height // block_rows, block_rows, -1))  10.4 us
    while x2, local copies, waits for them, and re-layouts  9.36 us
    concatenate x1, other arithmetic, block_power(): segments = jnp.concatenate([leading, trailing], axis=1)  7.56 us
    mul x2, other arithmetic, spectrum(): (last_real * last_real + closing_quadrature_part * closing_quadrature_par...  6.09 us
  transfers between devices with their start and end apart: 1, of which 1 were waited for; matrix products, arithmetic and copies ran while one was open for 1% of the time, Pallas kernels for 0%

commit v1 on v0

v1 whole, which is shorter than its diff:
```python
import jax
import jax.numpy as jnp
import numpy as np
from jax import lax
from jax.experimental import pallas as pl
from jax.experimental.pallas import tpu as pltpu
from jax.sharding import PartitionSpec as P

RADIX = 128
KBANDS = 33
SEG = RADIX * RADIX
HALF = SEG // 2
CHIPS = 8
ROWS = 40
MESH = pl.DeviceIdType.MESH
f32, bf16 = jnp.float32, jnp.bfloat16


def make_tables():
    a, k, m = np.arange(RADIX), np.arange(RADIX // 2), np.arange(RADIX)
    turn = 2 * np.pi
    inner = turn * ((k[:, None] * a[None, :]) % RADIX) / RADIX
    dft_in = np.concatenate([np.cos(inner), -np.sin(inner)])
    dft_in[RADIX // 2] = np.cos(np.pi * a)
    angle = turn * (k[:, None] * m[None, :]) / SEG
    real, imag = np.cos(angle), -np.sin(angle)
    real_b = real.copy()
    real_b[0] = 0
    mirror = turn * (((RADIX - k)[:, None] * m[None, :]) % SEG) / SEG
    m_real, m_imag = np.cos(mirror), -np.sin(mirror)
    angle_64 = turn * (RADIX // 2) * m / SEG
    p1, p2, p3, p4 = m_real.copy(), m_imag.copy(), m_imag.copy(), m_real.copy()
    p1[0], p2[0], p3[0], p4[0] = 0, np.cos(angle_64), 0, np.sin(angle_64)
    twiddle = np.stack([real, imag, real_b, p1, p2, p3, p4])
    j = np.arange(KBANDS)
    outer = turn * ((j[:, None] * m[None, :]) % RADIX) / RADIX
    cos, sin = np.cos(outer), np.sin(outer)
    dft_out = np.zeros((2 * ROWS, 2 * RADIX))
    dft_out[:KBANDS, :RADIX], dft_out[:KBANDS, RADIX:] = cos, sin
    dft_out[ROWS : ROWS + KBANDS, :RADIX], dft_out[ROWS : ROWS + KBANDS, RADIX:] = -sin, cos
    window = (0.5 - 0.5 * np.cos(turn * np.arange(SEG) / SEG)).reshape(RADIX, RADIX)
    norm = float(np.sum(window * window))
    single = lambda t: np.asarray(t, np.float32)
    return (
        single(dft_in).astype(jnp.bfloat16),
        single(dft_out).astype(jnp.bfloat16),
        single(twiddle),
        single(window),
        norm,
    )


def kernel(
    norm, x_ref, valid_ref, dft_in, dft_out, tw, win, out_ref,
    buf, halo, vloc, vpair, vhalo, vf, blocks, sums, tot, snd, rcv, fin,
    own_sem, pair_send, pair_recv, halo_send, halo_recv,
    v_send, v_recv, part_send, part_recv,
):
    me = lax.axis_index("chan")
    chip, core = me // 2, me % 2
    nxt, prv = (chip + 1) % CHIPS, (chip + CHIPS - 1) % CHIPS

    def chan(c, h):
        return {"chan": c * 2 + h}

    def slab_of(c, p):
        return (c + 2 * p + 1 - 7 * (p // 4)) % CHIPS

    def rows(g, h):
        return pl.ds(pl.multiple_of(g * 16 + h * 8, 8), 8)

    def own_copy(g):
        return pltpu.make_async_copy(x_ref.at[rows(g, core)], buf.at[core, g], own_sem.at[g])

    def remote(src, dst, send, recv, where):
        return pltpu.make_async_remote_copy(
            src_ref=src, dst_ref=dst, send_sem=send, recv_sem=recv,
            device_id=where, device_id_type=MESH,
        )

    def pair_copy(g, slot):
        return remote(
            x_ref.at[rows(g, 1 - core)], buf.at[slot, g],
            pair_send.at[g], pair_recv.at[g], chan(chip, 1 - core),
        )

    def halo_copy(g, h):
        return remote(
            x_ref.at[rows(g, h), pl.ds(HALF, HALF)], halo.at[g],
            halo_send.at[g, h], halo_recv.at[g], chan(nxt, h),
        )

    def part_copy(g, slot):
        return remote(snd.at[g], rcv.at[slot], part_send.at[g], part_recv.at[slot], chan(g, core))

    barrier = pltpu.get_barrier_semaphore()
    pl.semaphore_signal(barrier, 1, device_id=chan(chip, 1 - core), device_id_type=MESH)
    for d in range(1, CHIPS):
        pl.semaphore_signal(barrier, 1, device_id=chan((chip + d) % CHIPS, core), device_id_type=MESH)

    @pl.when(core == 0)
    def _():
        pl.semaphore_signal(barrier, 1, device_id=chan(prv, 1), device_id_type=MESH)

    def start_own(p, c):
        own_copy(slab_of(chip, p)).start()
        return c

    lax.fori_loop(0, CHIPS, start_own, 0)
    seen = valid_ref[...].astype(f32)
    for t in range(2):
        wide = jnp.broadcast_to(seen[:, t : t + 1], (RADIX, RADIX)).reshape(CHIPS, 2, 8, RADIX)
        for h in range(2):
            vloc[t, h] = wide[:, h].reshape(64, RADIX).astype(bf16)
    pl.semaphore_wait(barrier, CHIPS + core)

    v_pair = [
        remote(vloc.at[t, 1 - core], vpair.at[t], v_send.at[t], v_recv.at[t], chan(chip, 1 - core))
        for t in range(2)
    ]
    v_halo = [remote(vloc.at[1, h], vhalo, v_send.at[2 + h], v_recv.at[2], chan(nxt, h)) for h in range(2)]

    def start_copies(p, c):
        pair_copy(slab_of(chip, p), core).start()

        @pl.when(core == 1)
        def _():
            for h in range(2):
                halo_copy(slab_of(nxt, p), h).start()

        return c

    for copy in v_pair:
        copy.start()

    @pl.when(core == 1)
    def _():
        for copy in v_halo:
            copy.start()

    lax.fori_loop(0, CHIPS, start_copies, 0)

    def unpack(b, g, src, lanes):
        acc = jnp.zeros((8, RADIX), f32)
        for a in range(64):
            piece = src[:, lanes + a * RADIX : lanes + (a + 1) * RADIX].astype(f32)
            blocks[b, g, a * 8 : (a + 1) * 8, :] = piece
            acc = acc + piece
        sums[b, g] = jnp.broadcast_to(jnp.sum(acc, axis=1, keepdims=True), (8, RADIX))

    def segment(t, g):
        mean = (sums[t, g] + sums[t + 1, g]) * (1.0 / SEG)
        weight = vf[t, pl.ds(pl.multiple_of(g * 8, 8), 8), :]
        for c2 in range(4):
            shaped = []
            for c in (2 * c2, 2 * c2 + 1):
                mu = mean[c : c + 1, :]
                lead = (blocks[t, g, pl.ds(c, 64, stride=8), :] - mu) * win[0:64, :]
                trail = (blocks[t + 1, g, pl.ds(c, 64, stride=8), :] - mu) * win[64:128, :]
                shaped.append(jnp.concatenate([lead.astype(bf16), trail.astype(bf16)], axis=0))
            first = jnp.dot(dft_in[...], jnp.concatenate(shaped, axis=1), preferred_element_type=f32)
            middle = []
            for h in range(2):
                re = first[0:64, h * RADIX : (h + 1) * RADIX]
                im = first[64:128, h * RADIX : (h + 1) * RADIX]
                low = [re * tw[0] - im * tw[1], re * tw[1] + im * tw[2]]
                high = [re * tw[3] + im * tw[4], re * tw[5] - im * tw[6]]
                for pair in (low, high):
                    middle.append(jnp.concatenate([part.astype(bf16) for part in pair], axis=1))
            last = lax.dot_general(
                dft_out[...], jnp.concatenate(middle, axis=0),
                (((1,), (1,)), ((), ())), preferred_element_type=f32,
            )
            re, im = last[0:ROWS], last[ROWS : 2 * ROWS]
            scale = jnp.concatenate([weight[2 * c2 : 2 * c2 + 1], weight[2 * c2 + 1 : 2 * c2 + 2]], axis=1)
            tot[g, :, c2 * 256 : (c2 + 1) * 256] += (re * re + im * im) * scale

    for copy in v_pair:
        copy.wait_recv()
    mine = [vloc[t, core].astype(f32) for t in range(2)]
    other = [vpair[t].astype(f32) for t in range(2)]
    first_core = core == 0
    vf[1] = jnp.where(first_core, mine[0], other[0])
    vf[2] = jnp.where(first_core, mine[1], other[1])
    vf[3] = jnp.where(first_core, other[0], mine[0])

    def local(p, c):
        g = slab_of(chip, p)
        own_copy(g).wait()
        pair_copy(g, 1 - core).wait_recv()
        for b in range(4):
            unpack(b + 1, g, buf.at[b // 2, g], (b % 2) * HALF)
        tot[g] = jnp.zeros((ROWS, 1024), f32)

        def one(t, c):
            segment(t, g)
            return c

        return lax.fori_loop(1, 4, one, c)

    lax.fori_loop(0, CHIPS, local, 0)

    @pl.when(chip == 0)
    def _():
        def clear(g, c):
            blocks[1, g] = jnp.zeros((512, RADIX), f32)
            sums[1, g] = jnp.zeros((8, RADIX), f32)
            return c

        lax.fori_loop(0, CHIPS, clear, 0)

    v_halo[0].wait_recv()
    vf[0] = vhalo[...].astype(f32)

    def arrived(p, c):
        g = slab_of(chip, p)
        halo_copy(g, 0).wait_recv()
        unpack(0, g, halo.at[g], 0)
        segment(0, g)
        at = pl.ds(pl.multiple_of(g * 8, 8), 8)
        count = vf[0, at, :] + vf[1, at, :] + vf[2, at, :] + vf[3, at, :]
        tot[g, 33:34, :] = jnp.concatenate([count[c : c + 1] for c in range(8)], axis=1)
        snd[g] = tot[g].astype(bf16)

        @pl.when(p < CHIPS - 1)
        def _():
            part_copy(g, chip).start()

        return c

    lax.fori_loop(0, CHIPS, arrived, 0)

    fin[...] = tot[chip]

    def gather(p, c):
        s = slab_of(chip, p)
        part_copy(s, s).wait_recv()
        fin[...] += rcv[s].astype(f32)
        return c

    lax.fori_loop(0, CHIPS - 1, gather, 0)
    lane = lax.broadcasted_iota(jnp.int32, (ROWS, RADIX), 1)
    row = lax.broadcasted_iota(jnp.int32, (ROWS, RADIX), 0)
    scale = jnp.where((lane == 0) & (row == 0), 1.0, 2.0) * (1.0 / norm)
    order = jnp.where(lane <= 64, lane, 192 - lane)
    for c in range(8):
        power = fin[:, c * RADIX : (c + 1) * RADIX]
        average = power * scale / jnp.maximum(power[33:34, :], 1.0)
        average = jnp.take_along_axis(average, order, axis=1)
        sums_out = blocks.at[0, 0]
        sums_out[pl.ds(c, KBANDS, stride=8), :] = average[0:KBANDS]
    for j in range(KBANDS):
        out_ref[:, j * RADIX : (j + 1) * RADIX] = blocks[0, 0, j * 8 : (j + 1) * 8, :]

    def drain(p, c):
        g = slab_of(chip, p)
        pair_copy(g, core).wait_send()

        @pl.when(p < CHIPS - 1)
        def _():
            part_copy(g, chip).wait_send()

        @pl.when(core == 1)
        def _():
            for h in range(2):
                halo_copy(g, h).wait_send()

        return c

    lax.fori_loop(0, CHIPS, drain, 0)
    for copy in v_pair:
        copy.wait_send()

    @pl.when(core == 1)
    def _():
        for copy in v_halo:
            copy.wait_send()


def per_device(samples, valid):
    dft_in, dft_out, twiddle, window, norm = make_tables()
    vmem = pl.BlockSpec(memory_space=pltpu.VMEM)
    dma = pltpu.SemaphoreType.DMA
    return pl.pallas_call(
        lambda *refs: kernel(norm, *refs),
        out_shape=jax.ShapeDtypeStruct((8, KBANDS * RADIX), f32),
        in_specs=[pl.BlockSpec(memory_space=pl.ANY)] + [vmem] * 5,
        out_specs=vmem,
        scratch_shapes=[
            pltpu.VMEM((2, CHIPS, 8, SEG), bf16),
            pltpu.VMEM((CHIPS, 8, HALF), bf16),
            pltpu.VMEM((2, 2, 64, RADIX), bf16),
            pltpu.VMEM((2, 64, RADIX), bf16),
            pltpu.VMEM((64, RADIX), bf16),
            pltpu.VMEM((4, 64, RADIX), f32),
            pltpu.VMEM((5, CHIPS, 512, RADIX), f32),
            pltpu.VMEM((5, CHIPS, 8, RADIX), f32),
            pltpu.VMEM((CHIPS, ROWS, 1024), f32),
            pltpu.VMEM((CHIPS, ROWS, 1024), bf16),
            pltpu.VMEM((CHIPS, ROWS, 1024), bf16),
            pltpu.VMEM((ROWS, 1024), f32),
            dma((CHIPS,)), dma((CHIPS,)), dma((CHIPS,)), dma((CHIPS, 2)), dma((CHIPS,)),
            dma((4,)), dma((3,)), dma((CHIPS,)), dma((CHIPS,)),
        ],
        compiler_params=pltpu.CompilerParams(
            collective_id=0, has_side_effects=True, vmem_limit_bytes=56 * 2**20
        ),
    )(samples, valid, dft_in, dft_out, twiddle, window)


def solution(mesh):
    return jax.shard_map(
        per_device,
        mesh=mesh,
        in_specs=(P("tm", "chan"), P("tm", "chan")),
        out_specs=P(("tm", "chan"), None),
        check_vma=False,
    )
```

time: 191 us -> 46.2 us (0.24)
  local copies, waits for them, and re-layouts: 55.3 us -> 2.98 us
  waiting for transfers between devices: 49 us -> 0 us
  Pallas kernels: 0 us -> 43 us
  other arithmetic: 33.2 us -> 0 us
  matrix products: 30.6 us -> 0 us
  blocking collectives: 16.3 us -> 0 us
  starting transfers between devices: 4.93 us -> 0 us
    all_to_all x1 -> x0, waiting for transfers between devices: 49 us -> none  [per_device(): lax.all_to_all(samples, 'chan', split_axis=0, concat_axis=1, tiled=True)]
    pallas_call x0 -> x1, Pallas kernels: none -> 43 us  [per_device(): pl.pallas_call(lambda *refs: kernel(norm, *refs), out_shape=jax.ShapeDtyp...]
    dot_general x12 -> x0, matrix products: 30.6 us -> none  [contract(): return jnp.einsum(form, left, right, preferred_element_type=jnp.float32)]
    convert_element_type x3 -> x0, local copies, waits for them, and re-layouts: 18.7 us -> none  [the longest x2 18 us: spectrum(): values = segment.astype(jnp.float32)]
    all_to_all x1 -> x0, blocking collectives: 16.3 us -> none  [per_device(): lax.all_to_all(valid.astype(jnp.bfloat16), 'chan', split_axis=0, concat_a...]
    dynamic_update_slice x4 -> x0, local copies, waits for them, and re-layouts: 10.4 us -> none  [block_power(): lax.map(one_block, segments.reshape(height // block_rows, block_rows, -1))]
    slice x3 -> x0, local copies, waits for them, and re-layouts: 9.45 us -> none  [the longest x2 5.18 us: per_device(): leading = blocks[:, :-1].reshape(-1, half_len)]
    while x2 -> x0, local copies, waits for them, and re-layouts: 9.36 us -> none
  transfers between devices with their start and end apart: 1 -> 0, of which waited for: 1 -> 0; matrix products, arithmetic and copies ran while one was open for 1% -> 0% of each run, Pallas kernels for 0% -> 0%
where the time goes in v1:
time: 46.2 us; the launch traced here: 46 us
  Pallas kernels  43 us (93%)
  local copies, waits for them, and re-layouts  2.98 us (6%)
    pallas_call x1, Pallas kernels, per_device(): pl.pallas_call(lambda *refs: kernel(norm, *refs), out_shape=jax.ShapeDtyp...  43 us
    unnamed x2, local copies, waits for them, and re-layouts  2.98 us

profile of v1, /device:TPU:1, one launch (start us, length us, event | category | flops | bytes accessed | tf_op | source)
XLA Modules:
  0.0 46.0 jit_solution(4084427424942203153)
XLA Ops:
  0.0 1.4 %copy.7.refs_1_ = s32[128,2]{1,0:T(8,128)} copy(s32[128,2]{0,1:T(2,128)} %param.7) | data formatting | bytes 2048 | tf_op args[1]
  1.4 43.0 %shard_map.64 = f32[8,4224]{1,0:T(8,128)} custom-call(bf16[128,16384]{1,0:T(8,128)(2,1)} %refs_0_.1, s32[128,2]{1,0:T(8,128)} %copy.7.refs_1_, bf16[128,128]{1,0:T(8,128)(2,1)} %constant.8.clone.refs_2_, bf16[80,256]{1,0:T(8,128)(2,1)} %constant.9.clone.refs_3_, f32[7,64,128]{2,1,0:T(8,128)} %constant.10.clone.refs_4_, f32[128,128]{1,0:T(8,128)} %constant.11.clone.refs_5_), custom_call_target="tpu_custom_call" | custom-call | tf_op jit(solution)/shard_map/pallas_call | solution.py:284
  44.4 1.6 %copy.9 = f32[8,4224]{1,0:T(8,128)} copy(f32[8,4224]{1,0:T(8,128)} %shard_map.64) | data formatting | bytes 270336
